TPU v7x, 512 devices: a whole 4x8x8 slice. The times are simulated.
512 devices in a mesh: segment: 4 (over x), dp: 128 (over y, z, core).
Axes of the slice: x: 4, y: 8, z: 8, core: 2. Of those that a mesh axis runs over, the one named last changes fastest.
Arguments:
- fwd_in: bfloat16 [2, 4, 128, 16, 32, 256], P(None, 'segment', 'dp'), may hold values from -6 to 6
- bwd_in: bfloat16 [4, 4, 128, 16, 32, 256], P(None, 'segment', 'dp'), may hold values from -6 to 6
- fresh: bfloat16 [2, 128, 16, 32, 256], P(None, 'dp'), may hold values from -6 to 6
- top_cot: bfloat16 [2, 128, 16, 32, 256], P(None, 'dp'), may hold values from -6 to 6
- conv_weight: bfloat16 [4, 256, 9, 256], P('segment', 'dp'), may hold values from -0.125 to 0.125
Outputs:
- fwd_out: bfloat16 [2, 4, 128, 16, 32, 256], P(None, 'segment', 'dp')
- bwd_out: bfloat16 [4, 4, 128, 16, 32, 256], P(None, 'segment', 'dp')
- weight_grad: float32 [4, 256, 9, 256], P('segment', 'dp')
All inputs are finite; a program needn't handle non-finite values.
Results may differ from a plain program's by a relative error of at most 0.0055.
Values may be sent and summed in bfloat16 or wider, within the bound.
A program may use at most 64 MiB of HBM per device.

v0:
```python
import jax
import jax.numpy as jnp
from jax import lax
from jax.sharding import PartitionSpec as P


def from_partner(x, axis, bit):
    return lax.ppermute(x, axis, [(i, i ^ 1 << bit) for i in range(lax.axis_size(axis))])


def passed_along(block, axis, distance):
    devices = range(lax.axis_size(axis))
    route = [(i - distance, i) for i in devices if i - distance in devices]
    return lax.ppermute(block, axis, route)


def border_send(tile, parity):
    return jnp.where(parity == 0, tile[:, -1], tile[:, 0])


def extend_rows(tile, received, parity):
    blank_row = jnp.zeros_like(received)
    above_row = jnp.where(parity == 1, received, blank_row)[:, None]
    below_row = jnp.where(parity == 0, received, blank_row)[:, None]
    stacked = jnp.concatenate([above_row, tile, below_row], axis=1)
    return jnp.pad(stacked, ((0, 0), (0, 0), (1, 1), (0, 0)))


def window_at(extended, row_off, col_off, height, width, amount):
    portion = extended[:, row_off : row_off + height, col_off : col_off + width, :]
    return portion.reshape(-1, amount)


def conv_part(extended, weight_piece, height, width):
    amount = weight_piece.shape[0]
    running = None
    for row_off in range(3):
        for col_off in range(3):
            product_term = jnp.dot(
                window_at(extended, row_off, col_off, height, width, amount),
                weight_piece[:, 3 * row_off + col_off, :],
                preferred_element_type=jnp.float32,
            )
            running = product_term if running is None else running + product_term
    return running


def conv_transposed(cot_ext, weight_piece, height, width):
    channels = cot_ext.shape[3]
    running = None
    for row_off in range(3):
        for col_off in range(3):
            window = cot_ext[
                :, 2 - row_off : 2 - row_off + height, 2 - col_off : 2 - col_off + width, :
            ].reshape(-1, channels)
            product_term = lax.dot_general(
                window,
                weight_piece[:, 3 * row_off + col_off, :],
                (((1,), (1,)), ((), ())),
                preferred_element_type=jnp.float32,
            )
            running = product_term if running is None else running + product_term
    return running


def grad_part(extended, cotangent, amount, height, width):
    cot_flat = cotangent.reshape(-1, cotangent.shape[3])
    listing = []
    for row_off in range(3):
        for col_off in range(3):
            window = window_at(extended, row_off, col_off, height, width, amount)
            listing.append(
                lax.dot_general(
                    window, cot_flat, (((0,), (0,)), ((), ())), preferred_element_type=jnp.float32
                )
            )
    return jnp.stack(listing, axis=1)


def shards(fwd_in, bwd_in, fresh, top_cot, conv_weight):
    parity = lax.axis_index("dp") % 2
    segment_pos = lax.axis_index("segment")
    last_segment = lax.axis_size("segment") - 1
    weight_shard = conv_weight[0]
    height = fwd_in.shape[3]
    width = fwd_in.shape[4]
    channels = fwd_in.shape[5]
    pixels_all = lax.axis_size("dp") * height * width
    full_weight = lax.all_gather(weight_shard, "dp", axis=0, tiled=True)

    def two_convs(ext_fwd, ext_rec):
        return (
            conv_part(ext_fwd, full_weight, height, width),
            conv_part(ext_rec, full_weight, height, width),
        )

    def back_conv(cot_ext):
        return conv_transposed(cot_ext, full_weight, height, width)

    def one_step(stream_pair, back_four):
        first_in = stream_pair[0]
        second_in = stream_pair[1]
        out_first = back_four[0]
        out_second = back_four[1]
        cot_first = back_four[2]
        cot_second = back_four[3]
        received = from_partner(
            (
                border_send(second_in, parity),
                border_send(out_first, parity),
                border_send(cot_second, parity),
            ),
            "dp",
            0,
        )
        ext_fwd = jnp.maximum(extend_rows(second_in, received[0], parity), 0)
        ext_rec = jnp.maximum(extend_rows(out_first, received[1], parity), 0)
        ext_cot = extend_rows(cot_second, received[2], parity)
        branch_fwd, branch_rec = two_convs(ext_fwd, ext_rec)
        tile_shape = first_in.shape
        new_second = (first_in.astype(jnp.float32) + branch_fwd.reshape(tile_shape)).astype(
            jnp.bfloat16
        )
        forward_pair = jnp.stack([second_in, new_second])
        rebuilt = (out_second.astype(jnp.float32) - branch_rec.reshape(tile_shape)).astype(
            jnp.bfloat16
        )
        through = back_conv(ext_cot).reshape(tile_shape)
        cot_rebuilt = (
            cot_first.astype(jnp.float32) + jnp.where(out_first > 0, through, 0.0)
        ).astype(jnp.bfloat16)
        message = jnp.stack([rebuilt, out_first, cot_second, cot_rebuilt])
        return (forward_pair, message, (ext_rec, cot_second))

    forward_one, message_one, first_terms = one_step(fwd_in[:, 0], bwd_in[:, 0])
    arrived_fwd = passed_along(forward_one, "segment", 1)
    arrived_back = passed_along(message_one, "segment", -1)
    pair_two = jnp.where(segment_pos == 0, fresh, arrived_fwd)
    four_two = jnp.where(
        segment_pos == last_segment, jnp.concatenate([forward_one, top_cot], axis=0), arrived_back
    )
    forward_two, message_two, second_terms = one_step(pair_two, four_two)
    shard_rows = weight_shard.shape[0]
    summed = lax.psum(
        grad_part(first_terms[0], first_terms[1], channels, height, width)
        + grad_part(second_terms[0], second_terms[1], channels, height, width),
        "dp",
    )
    owned = lax.dynamic_slice_in_dim(summed, lax.axis_index("dp") * shard_rows, shard_rows, 0)
    weight_grad = (owned * (2.0 * pixels_all) ** (-0.5))[None]
    return (forward_two[:, None], message_two[:, None], weight_grad)


def solution(mesh):
    in_specs = (
        P(None, "segment", "dp", None, None, None),
        P(None, "segment", "dp", None, None, None),
        P(None, "dp", None, None, None),
        P(None, "dp", None, None, None),
        P("segment", "dp", None, None),
    )
    out_specs = (
        P(None, "segment", "dp", None, None, None),
        P(None, "segment", "dp", None, None, None),
        P("segment", "dp", None, None),
    )
    return jax.shard_map(shards, mesh=mesh, in_specs=in_specs, out_specs=out_specs, check_vma=False)
```

profile of v0, /device:TPU:24, one launch (start us, length us, event | category | flops | bytes accessed | tf_op | source)
XLA Modules:
  0.0 387.7 jit_solution(14345244486883992187)
XLA Ops:
  7.2 1.4 copy.35
  8.7 1.8 slice_bitcast_fusion.4
  10.5 1.9 collective-permute-start
  13.4 2.4 collective-permute-start.3
  15.9 1.9 collective-permute-start.4
  20.7 1.0 fusion.17
  23.9 1.0 fusion.14
  28.8 1.2 fusion.45
  30.0 1.5 fusion.47
  31.5 67.2 %all-gather.3.cloned.1.call-done = bf16[1,256,9,256]{3,2,0,1:T(8,128)(2,1)} async-done(((bf16[1,2,9,256]{3,2,0,1:T(8,128)(2,1)}), bf16[1,256,9,256]{3,2,0,1:T(8,128)(2,1)}) %all-gather.3.cloned.1.call-update) | async-done | bytes 1179664 | tf_op jit(solution)/shard_map/all_gather | solution.py:89
  98.7 2.0 copy.51
  110.6 3.5 collective-permute-start.1
  116.2 9.5 %collective-permute-done.1 = bf16[2,1,16,32,256]{4,3,2,1,0:T(8,128)(2,1)S(1)} collective-permute-done((bf16[2,1,16,32,256]{4,3,2,1,0:T(8,128)(2,1)S(1)}, bf16[2,1,16,32,256]{4,3,2,1,0:T(8,128)(2,1)S(1)}, u32[]{:S(2)}, u32[]{:S(2)}) %collective-permute-start.1) | collective-permute-done | bytes 524320 | tf_op jit(solution)/shard_map/ppermute | solution.py:14
  125.8 1.9 collective-permute-start.2
  127.9 1.3 collective-permute-start.5
  132.8 23.3 %collective-permute-done.5 = bf16[4,1,16,32,256]{4,3,2,0,1:T(8,128)(2,1)S(1)} collective-permute-done((bf16[4,1,16,32,256]{4,3,2,0,1:T(8,128)(2,1)S(1)}, bf16[4,1,16,32,256]{4,3,2,0,1:T(8,128)(2,1)S(1)}, u32[]{:S(2)}, u32[]{:S(2)}) %collective-permute-start.5) | collective-permute-done | bytes 1048608 | tf_op jit(solution)/shard_map/ppermute | solution.py:14
  157.0 1.9 collective-permute-start.7
  159.0 2.6 collective-permute-start.6
  161.7 1.1 fusion.43
  165.8 1.1 convolution_add_fusion.13
  167.2 1.1 convolution_add_fusion.12
  168.6 1.1 convolution_add_fusion.11
  170.0 1.1 convolution_add_fusion.10
  171.4 1.1 convolution_add_fusion.9
  172.8 1.1 convolution_add_fusion.8
  174.3 1.9 convolution_add_fusion.7
  176.5 3.4 add.257
  179.9 1.2 copy-done.1
  181.2 1.3 convolution_add_fusion.6
  186.2 1.1 maximum_bitcast_fusion
  187.3 192.1 %all-reduce.8.cloned.1.call-done = f32[256,9,256]{2,0,1:T(8,128)} async-done(((f32[256,9,256]{2,0,1:T(8,128)}), f32[256,9,256]{2,0,1:T(8,128)}) %all-reduce.8.cloned.1.call-update) | async-done | bytes 2359312 | tf_op jit(solution)/shard_map/psum | solution.py:144
  379.4 1.5 multiply_bitcast_fusion
  (173 shorter events, 35.0 us)
Async XLA Ops:
  7.2 5.3 %copy-start.5 = (bf16[4,1,1,16,32,256]{5,4,3,2,1,0:T(8,128)(2,1)S(1)}, bf16[4,1,1,16,32,256]{5,4,3,2,1,0:T(8,128)(2,1)}, u32[]{:S(2)}) copy-start(bf16[4,1,1,16,32,256]{5,4,3,2,1,0:T(8,128)(2,1)} %param.6) | copy-start | bytes 3145732
  7.2 91.6 %all-gather.3.cloned.1.call-start = ((), (), s32[]{:S(2)}) async-start(), calls=%async_computation.1 | async-start | bytes 2113536 | tf_op jit(solution)/shard_map/all_gather | solution.py:89
  8.6 370.8 %all-reduce.8.cloned.1.call-start = ((), (), s32[]{:S(2)}) async-start(), calls=%async_computation | async-start | bytes 4718592 | tf_op jit(solution)/shard_map/psum | solution.py:144
  10.5 11.3 %collective-permute-start = (bf16[1,32,256]{2,1,0:T(8,128)(2,1)S(1)}, bf16[1,32,256]{2,1,0:T(8,128)(2,1)S(1)}, u32[]{:S(2)}, u32[]{:S(2)}) collective-permute-start(bf16[1,32,256]{2,1,0:T(8,128)(2,1)S(1)} %fusion.39), channel_id=1, source_target_pairs={{0,1},{1,0},{2,3},{3,2},{4,5},{5,4},{6,7},{7,6},{8,9},{9,8},{10,11... | collective-permute-start | bytes 49160 | tf_op jit(solution)/shard_map/ppermute | solution.py:8
  13.4 4.4 %collective-permute-start.3 = (bf16[1,32,256]{2,1,0:T(8,128)(2,1)S(1)}, bf16[1,32,256]{2,1,0:T(8,128)(2,1)S(1)}, u32[]{:S(2)}, u32[]{:S(2)}) collective-permute-start(bf16[1,32,256]{2,1,0:T(8,128)(2,1)S(1)} %fusion.37), channel_id=1, source_target_pairs={{0,1},{1,0},{2,3},{3,2},{4,5},{5,4},{6,7},{7,6},{8,9},{9,8},{10,11... | collective-permute-start | bytes 49160 | tf_op jit(solution)/shard_map/ppermute | solution.py:8
  15.9 3.1 collective-permute-start.4
  18.3 3.4 copy-start.2
  100.8 64.5 %copy-start = (bf16[1,256,9,256]{3,1,2,0:T(8,128)(2,1)}, bf16[1,256,9,256]{3,1,2,0:T(8,128)(2,1)S(1)}, u32[]{:S(2)}) copy-start(bf16[1,256,9,256]{3,1,2,0:T(8,128)(2,1)S(1)} %copy.51) | copy-start | bytes 3538948
  100.8 1.1 copy-start.17
  101.0 1.2 copy-start.24
  101.9 1.0 copy-start.23
  105.7 1.0 copy-start.21
  109.3 1.1 copy-start.31
  109.6 1.0 copy-start.27
  109.8 4.4 %copy-start.13 = (bf16[1,16,32,256]{3,2,1,0:T(8,128)(2,1)S(1)}, bf16[1,16,32,256]{3,2,1,0:T(8,128)(2,1)}, u32[]{:S(2)}) copy-start(bf16[1,16,32,256]{3,2,1,0:T(8,128)(2,1)} %get-tuple-element.47) | copy-start | bytes 786436
  110.6 3.9 %copy-start.12 = (bf16[1,16,32,256]{3,2,1,0:T(8,128)(2,1)S(1)}, bf16[1,16,32,256]{3,2,1,0:T(8,128)(2,1)}, u32[]{:S(2)}) copy-start(bf16[1,16,32,256]{3,2,1,0:T(8,128)(2,1)} %get-tuple-element.46) | copy-start | bytes 786436
  110.6 15.1 %collective-permute-start.1 = (bf16[2,1,16,32,256]{4,3,2,1,0:T(8,128)(2,1)S(1)}, bf16[2,1,16,32,256]{4,3,2,1,0:T(8,128)(2,1)S(1)}, u32[]{:S(2)}, u32[]{:S(2)}) collective-permute-start(bf16[2,1,16,32,256]{4,3,2,1,0:T(8,128)(2,1)S(1)} %pad_maximum_fusion.1), channel_id=1, source_target_pairs={{0,128},{128,256},{256,384},{1,129},{129,257},{257,385},{2,130},{1... | collective-permute-start | bytes 1572872 | tf_op jit(solution)/shard_map/ppermute | solution.py:14
  114.7 1.2 copy-start.6
  115.9 9.7 %copy-start.30 = (bf16[2,1,16,32,256]{4,3,2,1,0:T(8,128)(2,1)S(1)}, bf16[2,1,16,32,256]{4,3,2,1,0:T(8,128)(2,1)}, u32[]{:S(2)}) copy-start(bf16[2,1,16,32,256]{4,3,2,1,0:T(8,128)(2,1)} %param.7) | copy-start | bytes 1572868
  116.2 11.5 %copy-start.25 = (bf16[1,1,16,32,256]{4,3,2,0,1:T(8,128)(2,1)S(1)}, bf16[1,1,16,32,256]{4,3,2,0,1:T(8,128)(2,1)}, u32[]{:S(2)}) copy-start(bf16[1,1,16,32,256]{4,3,2,0,1:T(8,128)(2,1)} %get-tuple-element.12) | copy-start | bytes 786436
  116.2 11.5 %copy-start.26 = (bf16[1,1,16,32,256]{4,3,2,0,1:T(8,128)(2,1)S(1)}, bf16[1,1,16,32,256]{4,3,2,0,1:T(8,128)(2,1)}, u32[]{:S(2)}) copy-start(bf16[1,1,16,32,256]{4,3,2,0,1:T(8,128)(2,1)} %get-tuple-element.14) | copy-start | bytes 786436
  125.8 3.4 collective-permute-start.2
  127.9 28.2 %collective-permute-start.5 = (bf16[4,1,16,32,256]{4,3,2,0,1:T(8,128)(2,1)S(1)}, bf16[4,1,16,32,256]{4,3,2,0,1:T(8,128)(2,1)S(1)}, u32[]{:S(2)}, u32[]{:S(2)}) collective-permute-start(bf16[4,1,16,32,256]{4,3,2,0,1:T(8,128)(2,1)S(1)} %pad_maximum_fusion), channel_id=1, source_target_pairs={{128,0},{256,128},{384,256},{129,1},{257,129},{385,257},{130,2},{2... | collective-permute-start | bytes 3145736 | tf_op jit(solution)/shard_map/ppermute | solution.py:14
  131.8 24.3 %copy-start.29 = (bf16[1,1,16,32,256]{4,3,2,0,1:T(8,128)(2,1)S(1)}, bf16[1,1,16,32,256]{4,3,2,0,1:T(8,128)(2,1)}, u32[]{:S(2)}) copy-start(bf16[1,1,16,32,256]{4,3,2,0,1:T(8,128)(2,1)} %get-tuple-element.16) | copy-start | bytes 786436
  131.8 24.2 %copy-start.32 = (bf16[2,1,16,32,256]{4,3,2,1,0:T(8,128)(2,1)S(1)}, bf16[2,1,16,32,256]{4,3,2,1,0:T(8,128)(2,1)}, u32[]{:S(2)}) copy-start(bf16[2,1,16,32,256]{4,3,2,1,0:T(8,128)(2,1)} %param.8) | copy-start | bytes 1572868
  157.0 4.5 %collective-permute-start.7 = (bf16[1,32,256]{2,1,0:T(8,128)(2,1)S(1)}, bf16[1,32,256]{2,1,0:T(8,128)(2,1)S(1)}, u32[]{:S(2)}, u32[]{:S(2)}) collective-permute-start(bf16[1,32,256]{2,1,0:T(8,128)(2,1)S(1)} %fusion.34), channel_id=1, source_target_pairs={{0,1},{1,0},{2,3},{3,2},{4,5},{5,4},{6,7},{7,6},{8,9},{9,8},{10,11... | collective-permute-start | bytes 49160 | tf_op jit(solution)/shard_map/ppermute | solution.py:8
  159.0 5.3 %collective-permute-start.6 = (bf16[1,32,256]{2,1,0:T(8,128)(2,1)S(1)}, bf16[1,32,256]{2,1,0:T(8,128)(2,1)S(1)}, u32[]{:S(2)}, u32[]{:S(2)}) collective-permute-start(bf16[1,32,256]{2,1,0:T(8,128)(2,1)S(1)} %fusion.35), channel_id=1, source_target_pairs={{0,1},{1,0},{2,3},{3,2},{4,5},{5,4},{6,7},{7,6},{8,9},{9,8},{10,11... | collective-permute-start | bytes 49160 | tf_op jit(solution)/shard_map/ppermute | solution.py:8
  179.9 1.3 copy-start.1
  179.9 2.5 copy-start.11
  181.2 1.5 copy-start.9
  183.3 1.0 copy-start.10
  184.2 1.1 copy-start.4
  (11 other events, 10.6 us)
Sparse Core Ops, SparseCore 0:
  11.7 87.0 all-gather.2
  180.0 199.3 all-reduce.7
where the time goes:
time: 389 us; the launch traced here: 388 us
  waiting for transfers between devices  293 us (75%)
  matrix products  32.2 us (8%)
  local copies, waits for them, and re-layouts  19.8 us (5%)
  starting transfers between devices  17.6 us (5%)
  between operations  15 us (4%)
  other arithmetic  10.5 us (3%)
    psum x1, waiting for transfers between devices, shards(): lax.psum(grad_part(first_terms[0], first_terms[1], channels, height, widt...  192 us
    all_gather x1, waiting for transfers between devices, shards(): full_weight = lax.all_gather(weight_shard, 'dp', axis=0, tiled=True)  67.2 us
    ppermute x2, waiting for transfers between devices, passed_along(): return lax.ppermute(block, axis, route)  32.8 us
    dot_general x36, matrix products, conv_part(): jnp.dot(window_at(extended, row_off, col_off, height, width, amount), wei...  15.3 us
    ppermute x6, starting transfers between devices, from_partner(): lax.ppermute(x, axis, [(i, i ^ 1 << bit) for i in range(lax.axis_size(axi...  12.6 us
    dot_general x18, matrix products, grad_part(): lax.dot_general(window, cot_flat, (((0,), (0,)), ((), ())), preferred_ele...  11.3 us
    unnamed x67, local copies, waits for them, and re-layouts  9.48 us
  transfers between devices with their start and end apart: 10, of which 5 were waited for; matrix products, arithmetic and copies ran while one was open for 7% of the time, Pallas kernels for 0%

commit v1 on v0

--- a/solution.py
+++ b/solution.py
@@ -2,6 +2,7 @@
 import jax.numpy as jnp
 from jax import lax
 from jax.sharding import PartitionSpec as P
+from jax.lax import all_to_all, axis_size
 
 
 def from_partner(x, axis, bit):
@@ -86,7 +87,10 @@
     width = fwd_in.shape[4]
     channels = fwd_in.shape[5]
     pixels_all = lax.axis_size("dp") * height * width
-    full_weight = lax.all_gather(weight_shard, "dp", axis=0, tiled=True)
+    full_weight = jnp.concatenate(
+        all_to_all(jnp.stack([weight_shard for _ in range(axis_size("dp"))], axis=0), "dp", 0, 0),
+        axis=0,
+    )
 
     def two_convs(ext_fwd, ext_rec):
         return (

time: 389 us -> 353 us (0.907)
  waiting for transfers between devices: 293 us -> 234 us
  starting transfers between devices: 17.6 us -> 35.5 us
    all_gather x1 -> x0, waiting for transfers between devices: 67.2 us -> none  [shards(): full_weight = lax.all_gather(weight_shard, 'dp', axis=0, tiled=True)]
    all_to_all x0 -> x1, starting transfers between devices: none -> 17.6 us  [shards(): all_to_all(jnp.stack([weight_shard for _ in range(axis_size('dp'))], axis...]
    all_to_all x0 -> x1, waiting for transfers between devices: none -> 11.9 us  [shards(): all_to_all(jnp.stack([weight_shard for _ in range(axis_size('dp'))], axis...]
    unnamed x67 -> x96, local copies, waits for them, and re-layouts: 9.48 us -> 10.1 us
  transfers between devices with their start and end apart: 10 -> 10, of which waited for: 5 -> 5; matrix products, arithmetic and copies ran while one was open for 7% -> 8% of each run, Pallas kernels for 0% -> 0%
where the time goes in v1:
time: 353 us; the launch traced here: 352 us
  waiting for transfers between devices  234 us (66%)
  starting transfers between devices  35.5 us (10%)
  matrix products  33.4 us (9%)
  local copies, waits for them, and re-layouts  22.5 us (6%)
  between operations  15.1 us (4%)
  other arithmetic  10.7 us (3%)
    psum x1, waiting for transfers between devices, shards(): lax.psum(grad_part(first_terms[0], first_terms[1], channels, height, widt...  190 us
    ppermute x2, waiting for transfers between devices, passed_along(): return lax.ppermute(block, axis, route)  32.3 us
    all_to_all x1, starting transfers between devices, shards(): all_to_all(jnp.stack([weight_shard for _ in range(axis_size('dp'))], axis...  17.6 us
    dot_general x36, matrix products, conv_part(): jnp.dot(window_at(extended, row_off, col_off, height, width, amount), wei...  15.3 us
    ppermute x6, starting transfers between devices, from_partner(): lax.ppermute(x, axis, [(i, i ^ 1 << bit) for i in range(lax.axis_size(axi...  12.8 us
    all_to_all x1, waiting for transfers between devices, shards(): all_to_all(jnp.stack([weight_shard for _ in range(axis_size('dp'))], axis...  11.9 us
    dot_general x18, matrix products, grad_part(): lax.dot_general(window, cot_flat, (((0,), (0,)), ((), ())), preferred_ele...  11.2 us
    unnamed x96, local copies, waits for them, and re-layouts  10.1 us
  transfers between devices with their start and end apart: 10, of which 5 were waited for; matrix products, arithmetic and copies ran while one was open for 8% of the time, Pallas kernels for 0%

profile of v1, /device:TPU:24, one launch (start us, length us, event | category | flops | bytes accessed | tf_op | source)
XLA Modules:
  0.0 351.6 jit_solution(8918057782934696423)
XLA Ops:
  7.2 1.8 slice_bitcast_fusion.4
  9.7 1.9 collective-permute-start
  11.6 2.4 stack.81
  14.0 17.6 %all-to-all-start = ((bf16[128,2,9,256]{3,1,2,0:T(2,128)(2,1)}), bf16[128,2,9,256]{3,1,2,0:T(2,128)(2,1)S(1)}, u32[]{:S(2)}, u32[]{:S(2)}) async-start(bf16[128,2,9,256]{3,1,2,0:T(2,128)(2,1)} %stack.81), calls=%async_computation | async-start | bytes 2359296 | tf_op jit(solution)/shard_map/all_to_all | solution.py:91
  32.6 2.0 collective-permute-start.3
  34.6 2.3 collective-permute-start.4
  37.8 1.0 pad_maximum_fusion.4
  48.0 1.3 fusion.45
  49.3 1.6 fusion.47
  50.9 11.9 %all-to-all-done = bf16[128,2,9,256]{3,1,2,0:T(2,128)(2,1)S(1)} async-done(((bf16[128,2,9,256]{3,1,2,0:T(2,128)(2,1)}), bf16[128,2,9,256]{3,1,2,0:T(2,128)(2,1)S(1)}, u32[]{:S(2)}, u32[]{:S(2)}) %all-to-all-start) | async-done | bytes 1179680 | tf_op jit(solution)/shard_map/all_to_all | solution.py:91
  64.5 1.4 fusion.29
  76.2 3.6 %collective-permute-start.1 = (bf16[2,1,16,32,256]{4,3,2,1,0:T(8,128)(2,1)S(1)}, bf16[2,1,16,32,256]{4,3,2,1,0:T(8,128)(2,1)S(1)}, u32[]{:S(2)}, u32[]{:S(2)}) collective-permute-start(bf16[2,1,16,32,256]{4,3,2,1,0:T(8,128)(2,1)S(1)} %pad_maximum_fusion.1), channel_id=1, source_target_pairs={{0,128},{128,256},{256,384},{1,129},{129,257},{257,385},{2,130},{1... | collective-permute-start | bytes 1572872 | tf_op jit(solution)/shard_map/ppermute | solution.py:15
  82.1 9.6 %collective-permute-done.1 = bf16[2,1,16,32,256]{4,3,2,1,0:T(8,128)(2,1)S(1)} collective-permute-done((bf16[2,1,16,32,256]{4,3,2,1,0:T(8,128)(2,1)S(1)}, bf16[2,1,16,32,256]{4,3,2,1,0:T(8,128)(2,1)S(1)}, u32[]{:S(2)}, u32[]{:S(2)}) %collective-permute-start.1) | collective-permute-done | bytes 524320 | tf_op jit(solution)/shard_map/ppermute | solution.py:15
  91.9 2.3 collective-permute-start.2
  94.3 1.5 collective-permute-start.5
  99.4 22.7 %collective-permute-done.5 = bf16[4,1,16,32,256]{4,3,2,0,1:T(8,128)(2,1)S(1)} collective-permute-done((bf16[4,1,16,32,256]{4,3,2,0,1:T(8,128)(2,1)S(1)}, bf16[4,1,16,32,256]{4,3,2,0,1:T(8,128)(2,1)S(1)}, u32[]{:S(2)}, u32[]{:S(2)}) %collective-permute-start.5) | collective-permute-done | bytes 1048608 | tf_op jit(solution)/shard_map/ppermute | solution.py:15
  123.1 1.9 collective-permute-start.7
  125.0 2.4 collective-permute-start.6
  127.6 1.2 fusion.43
  131.7 1.1 convolution_add_fusion.13
  133.1 1.1 convolution_add_fusion.12
  134.5 1.1 convolution_add_fusion.11
  135.9 1.1 convolution_add_fusion.10
  137.4 1.1 convolution_add_fusion.9
  138.8 1.1 convolution_add_fusion.8
  140.2 1.9 convolution_add_fusion.7
  142.4 3.4 add.257
  145.9 1.2 copy-done.1
  147.1 1.3 convolution_add_fusion.6
  152.2 1.1 maximum_bitcast_fusion
  153.3 190.0 %all-reduce.8.cloned.1.call-done = f32[256,9,256]{2,0,1:T(8,128)} async-done(((f32[256,9,256]{2,0,1:T(8,128)}), f32[256,9,256]{2,0,1:T(8,128)}) %all-reduce.8.cloned.1.call-update) | async-done | bytes 2359312 | tf_op jit(solution)/shard_map/psum | solution.py:148
  343.3 1.5 multiply_bitcast_fusion
  (203 shorter events, 39.0 us)
Async XLA Ops:
  9.7 31.2 %collective-permute-start = (bf16[1,32,256]{2,1,0:T(8,128)(2,1)S(1)}, bf16[1,32,256]{2,1,0:T(8,128)(2,1)S(1)}, u32[]{:S(2)}, u32[]{:S(2)}) collective-permute-start(bf16[1,32,256]{2,1,0:T(8,128)(2,1)S(1)} %fusion.39), channel_id=1, source_target_pairs={{0,1},{1,0},{2,3},{3,2},{4,5},{5,4},{6,7},{7,6},{8,9},{9,8},{10,11... | collective-permute-start | bytes 49160 | tf_op jit(solution)/shard_map/ppermute | solution.py:9
  14.0 17.6 %copy-start.15 = (bf16[4,1,1,16,32,256]{5,4,3,2,1,0:T(8,128)(2,1)S(1)}, bf16[4,1,1,16,32,256]{5,4,3,2,1,0:T(8,128)(2,1)}, u32[]{:S(2)}) copy-start(bf16[4,1,1,16,32,256]{5,4,3,2,1,0:T(8,128)(2,1)} %param.6) | copy-start | bytes 3145732
  14.0 48.8 %all-to-all-start = ((bf16[128,2,9,256]{3,1,2,0:T(2,128)(2,1)}), bf16[128,2,9,256]{3,1,2,0:T(2,128)(2,1)S(1)}, u32[]{:S(2)}, u32[]{:S(2)}) async-start(bf16[128,2,9,256]{3,1,2,0:T(2,128)(2,1)} %stack.81), calls=%async_computation | async-start | bytes 2359296 | tf_op jit(solution)/shard_map/all_to_all | solution.py:91
  31.6 311.7 %all-reduce.8.cloned.1.call-start = ((), (), s32[]{:S(2)}) async-start(), calls=%async_computation.1 | async-start | bytes 4718592 | tf_op jit(solution)/shard_map/psum | solution.py:148
  32.6 4.4 %collective-permute-start.3 = (bf16[1,32,256]{2,1,0:T(8,128)(2,1)S(1)}, bf16[1,32,256]{2,1,0:T(8,128)(2,1)S(1)}, u32[]{:S(2)}, u32[]{:S(2)}) collective-permute-start(bf16[1,32,256]{2,1,0:T(8,128)(2,1)S(1)} %fusion.37), channel_id=1, source_target_pairs={{0,1},{1,0},{2,3},{3,2},{4,5},{5,4},{6,7},{7,6},{8,9},{9,8},{10,11... | collective-permute-start | bytes 49160 | tf_op jit(solution)/shard_map/ppermute | solution.py:9
  34.6 3.1 collective-permute-start.4
  37.5 3.3 copy-start.12
  37.5 3.6 %copy-start.10 = (bf16[1,16,32,256]{3,2,1,0:T(8,128)(2,1)}, bf16[1,16,32,256]{3,2,1,0:T(8,128)(2,1)S(1)}, u32[]{:S(2)}) copy-start(bf16[1,16,32,256]{3,2,1,0:T(8,128)(2,1)S(1)} %get-tuple-element.42) | copy-start | bytes 786436
  37.5 4.6 %copy-start.8 = (bf16[1,16,32,256]{3,2,1,0:T(8,128)(2,1)}, bf16[1,16,32,256]{3,2,1,0:T(8,128)(2,1)S(1)}, u32[]{:S(2)}) copy-start(bf16[1,16,32,256]{3,2,1,0:T(8,128)(2,1)S(1)} %get-tuple-element.41) | copy-start | bytes 786436
  37.5 5.6 %copy-start.6 = (bf16[1,16,32,256]{3,2,1,0:T(8,128)(2,1)}, bf16[1,16,32,256]{3,2,1,0:T(8,128)(2,1)S(1)}, u32[]{:S(2)}) copy-start(bf16[1,16,32,256]{3,2,1,0:T(8,128)(2,1)S(1)} %get-tuple-element.40) | copy-start | bytes 786436
  37.5 6.5 %copy-start.4 = (bf16[1,16,32,256]{3,2,1,0:T(8,128)(2,1)}, bf16[1,16,32,256]{3,2,1,0:T(8,128)(2,1)S(1)}, u32[]{:S(2)}) copy-start(bf16[1,16,32,256]{3,2,1,0:T(8,128)(2,1)S(1)} %get-tuple-element.39) | copy-start | bytes 786436
  37.5 7.5 %copy-start.2 = (bf16[1,16,32,256]{3,2,1,0:T(8,128)(2,1)}, bf16[1,16,32,256]{3,2,1,0:T(8,128)(2,1)S(1)}, u32[]{:S(2)}) copy-start(bf16[1,16,32,256]{3,2,1,0:T(8,128)(2,1)S(1)} %get-tuple-element.38) | copy-start | bytes 786436
  38.8 2.1 copy-start.18
  64.2 67.0 %copy-start = (bf16[256,9,256]{2,0,1:T(8,128)(2,1)}, bf16[256,9,256]{2,0,1:T(8,128)(2,1)S(1)}, u32[]{:S(2)}) copy-start(bf16[256,9,256]{2,0,1:T(8,128)(2,1)S(1)} %reshape.497) | copy-start | bytes 3538948
  64.2 1.7 copy-start.32
  64.4 1.8 copy-start.39
  75.3 4.4 %copy-start.28 = (bf16[1,16,32,256]{3,2,1,0:T(8,128)(2,1)S(1)}, bf16[1,16,32,256]{3,2,1,0:T(8,128)(2,1)}, u32[]{:S(2)}) copy-start(bf16[1,16,32,256]{3,2,1,0:T(8,128)(2,1)} %get-tuple-element.47) | copy-start | bytes 786436
  76.1 3.9 %copy-start.25 = (bf16[1,16,32,256]{3,2,1,0:T(8,128)(2,1)S(1)}, bf16[1,16,32,256]{3,2,1,0:T(8,128)(2,1)}, u32[]{:S(2)}) copy-start(bf16[1,16,32,256]{3,2,1,0:T(8,128)(2,1)} %get-tuple-element.46) | copy-start | bytes 786436
  76.2 15.6 %collective-permute-start.1 = (bf16[2,1,16,32,256]{4,3,2,1,0:T(8,128)(2,1)S(1)}, bf16[2,1,16,32,256]{4,3,2,1,0:T(8,128)(2,1)S(1)}, u32[]{:S(2)}, u32[]{:S(2)}) collective-permute-start(bf16[2,1,16,32,256]{4,3,2,1,0:T(8,128)(2,1)S(1)} %pad_maximum_fusion.1), channel_id=1, source_target_pairs={{0,128},{128,256},{256,384},{1,129},{129,257},{257,385},{2,130},{1... | collective-permute-start | bytes 1572872 | tf_op jit(solution)/shard_map/ppermute | solution.py:15
  80.7 1.2 copy-start.16
  81.9 9.8 %copy-start.45 = (bf16[2,1,16,32,256]{4,3,2,1,0:T(8,128)(2,1)S(1)}, bf16[2,1,16,32,256]{4,3,2,1,0:T(8,128)(2,1)}, u32[]{:S(2)}) copy-start(bf16[2,1,16,32,256]{4,3,2,1,0:T(8,128)(2,1)} %param.7) | copy-start | bytes 1572868
  82.1 12.0 %copy-start.40 = (bf16[1,1,16,32,256]{4,3,2,0,1:T(8,128)(2,1)S(1)}, bf16[1,1,16,32,256]{4,3,2,0,1:T(8,128)(2,1)}, u32[]{:S(2)}) copy-start(bf16[1,1,16,32,256]{4,3,2,0,1:T(8,128)(2,1)} %get-tuple-element.12) | copy-start | bytes 786436
  82.1 12.0 %copy-start.41 = (bf16[1,1,16,32,256]{4,3,2,0,1:T(8,128)(2,1)S(1)}, bf16[1,1,16,32,256]{4,3,2,0,1:T(8,128)(2,1)}, u32[]{:S(2)}) copy-start(bf16[1,1,16,32,256]{4,3,2,0,1:T(8,128)(2,1)} %get-tuple-element.14) | copy-start | bytes 786436
  91.9 3.9 %collective-permute-start.2 = (bf16[1,32,256]{2,1,0:T(8,128)(2,1)S(1)}, bf16[1,32,256]{2,1,0:T(8,128)(2,1)S(1)}, u32[]{:S(2)}, u32[]{:S(2)}) collective-permute-start(bf16[1,32,256]{2,1,0:T(8,128)(2,1)S(1)} %fusion.38), channel_id=1, source_target_pairs={{0,1},{1,0},{2,3},{3,2},{4,5},{5,4},{6,7},{7,6},{8,9},{9,8},{10,11... | collective-permute-start | bytes 49160 | tf_op jit(solution)/shard_map/ppermute | solution.py:9
  94.3 27.8 %collective-permute-start.5 = (bf16[4,1,16,32,256]{4,3,2,0,1:T(8,128)(2,1)S(1)}, bf16[4,1,16,32,256]{4,3,2,0,1:T(8,128)(2,1)S(1)}, u32[]{:S(2)}, u32[]{:S(2)}) collective-permute-start(bf16[4,1,16,32,256]{4,3,2,0,1:T(8,128)(2,1)S(1)} %pad_maximum_fusion), channel_id=1, source_target_pairs={{128,0},{256,128},{384,256},{129,1},{257,129},{385,257},{130,2},{2... | collective-permute-start | bytes 3145736 | tf_op jit(solution)/shard_map/ppermute | solution.py:15
  98.4 23.7 %copy-start.44 = (bf16[1,1,16,32,256]{4,3,2,0,1:T(8,128)(2,1)S(1)}, bf16[1,1,16,32,256]{4,3,2,0,1:T(8,128)(2,1)}, u32[]{:S(2)}) copy-start(bf16[1,1,16,32,256]{4,3,2,0,1:T(8,128)(2,1)} %get-tuple-element.16) | copy-start | bytes 786436
  98.5 23.7 %copy-start.47 = (bf16[2,1,16,32,256]{4,3,2,1,0:T(8,128)(2,1)S(1)}, bf16[2,1,16,32,256]{4,3,2,1,0:T(8,128)(2,1)}, u32[]{:S(2)}) copy-start(bf16[2,1,16,32,256]{4,3,2,1,0:T(8,128)(2,1)} %param.8) | copy-start | bytes 1572868
  123.1 4.3 %collective-permute-start.7 = (bf16[1,32,256]{2,1,0:T(8,128)(2,1)S(1)}, bf16[1,32,256]{2,1,0:T(8,128)(2,1)S(1)}, u32[]{:S(2)}, u32[]{:S(2)}) collective-permute-start(bf16[1,32,256]{2,1,0:T(8,128)(2,1)S(1)} %fusion.34), channel_id=1, source_target_pairs={{0,1},{1,0},{2,3},{3,2},{4,5},{5,4},{6,7},{7,6},{8,9},{9,8},{10,11... | collective-permute-start | bytes 49160 | tf_op jit(solution)/shard_map/ppermute | solution.py:9
  125.0 5.1 %collective-permute-start.6 = (bf16[1,32,256]{2,1,0:T(8,128)(2,1)S(1)}, bf16[1,32,256]{2,1,0:T(8,128)(2,1)S(1)}, u32[]{:S(2)}, u32[]{:S(2)}) collective-permute-start(bf16[1,32,256]{2,1,0:T(8,128)(2,1)S(1)} %fusion.35), channel_id=1, source_target_pairs={{0,1},{1,0},{2,3},{3,2},{4,5},{5,4},{6,7},{7,6},{8,9},{9,8},{10,11... | collective-permute-start | bytes 49160 | tf_op jit(solution)/shard_map/ppermute | solution.py:9
  145.8 1.3 copy-start.1
  145.8 2.5 copy-start.27
  147.1 1.5 copy-start.24
  (26 other events, 25.0 us)
Sparse Core Ops, SparseCore 0:
  146.0 197.2 all-reduce.7
